TPU v7x, 128 devices: a whole 4x4x4 slice. The times are simulated.
128 devices in a mesh: patch: 16 (over z, x_lo, core), head: 8 (over y, x_hi).
Axes of the slice: x: 4 (x_hi: 2, x_lo: 2; x = x_hi * 2 + x_lo), y: 4, z: 4, core: 2. Of those that a mesh axis runs over, the one named last changes fastest.
Arguments:
- img_qkv: bfloat16 [8192, 9216], P(('patch', 'head')), may hold values from -8 to 8
- txt_qkv: bfloat16 [512, 9216], P('head'), may hold values from -8 to 8
- stale_kv: bfloat16 [2, 8192, 3072], P(None, 'patch', 'head'), may hold values from -8 to 8
- residual: bfloat16 [8192, 3072], P(('patch', 'head')), may hold values from -4 to 4
- gate_scale: float32 [3072], replicated, may hold values from 0.5 to 3
- proj_weight: bfloat16 [3072, 3072], replicated, may hold values from -0.109375 to 0.109375
Outputs:
- image_out: bfloat16 [8192, 3072], P(('patch', 'head'))
- text_attn: bfloat16 [512, 3072], P('head')
All inputs are finite; a program needn't handle non-finite values.
Results may differ from a plain program's by a relative error of at most 0.0075.
Values may be sent and summed in bfloat16 or wider, within the bound.
A program may use at most 192 MiB of HBM per device.

v0:
```python
import math
import jax
import jax.numpy as jnp
from jax import lax
from jax.sharding import PartitionSpec as P

HD = 128


def block_stats(queries, key_rows, values):
    scores = jnp.einsum("rhd,khd->rhk", queries, key_rows, preferred_element_type=jnp.float32) * (
        1.0 / math.sqrt(HD)
    )
    row_max = jnp.max(scores, axis=2)
    shifted = jnp.exp(scores - row_max[:, :, None])
    row_sum = jnp.sum(shifted, axis=2)
    weighted = jnp.einsum(
        "rhk,khd->rhd", shifted.astype(jnp.bfloat16), values, preferred_element_type=jnp.float32
    )
    return (row_max, row_sum, weighted)


def combine(first, second):
    joint_max = jnp.maximum(first[0], second[0])
    first_scale = jnp.exp(first[0] - joint_max)
    second_scale = jnp.exp(second[0] - joint_max)
    return (
        joint_max,
        first[1] * first_scale + second[1] * second_scale,
        first[2] * first_scale[:, :, None] + second[2] * second_scale[:, :, None],
    )


def finish(totals):
    return (totals[2] / totals[1][:, :, None]).astype(jnp.bfloat16)


def per_device(img_qkv, txt_qkv, stale_kv, residual, gate_scale, proj_weight):
    my_group = lax.axis_index("patch")
    img_rows = img_qkv.shape[0]
    model_width = img_qkv.shape[1] // 3
    head_count = model_width // HD
    img_split = img_qkv.reshape(img_rows, 3, head_count, HD)
    txt_split = txt_qkv.reshape(txt_qkv.shape[0], 3, head_count, HD)
    img_heads, txt_heads = (
        lax.all_to_all(img_split, "head", split_axis=2, concat_axis=0, tiled=True),
        lax.all_to_all(txt_split, "head", split_axis=2, concat_axis=0, tiled=True),
    )
    query_img = img_heads[:, 0]
    keys_img = img_heads[:, 1]
    values_img = img_heads[:, 2]
    query_txt = txt_heads[:, 0]
    keys_txt = txt_heads[:, 1]
    values_txt = txt_heads[:, 2]
    group_rows = query_img.shape[0]
    local_heads = query_img.shape[1]
    image_init = block_stats(query_img, keys_txt, values_txt)
    text_init = block_stats(query_txt, keys_txt, values_txt)
    own_first = my_group * group_rows
    shard_rows = lax.all_gather(stale_kv, "patch", axis=1, tiled=True)
    shard_count = shard_rows.shape[1] // group_rows
    key_blocks = jnp.moveaxis(shard_rows.reshape(2, shard_count, group_rows, local_heads, HD), 1, 0)
    starts = group_rows * jnp.arange(shard_count, dtype=jnp.int32)

    def one_block(running_pair, inputs):
        key_block, block_first = inputs
        is_fresh = block_first == own_first
        key_rows = jnp.where(is_fresh, keys_img, key_block[0])
        values = jnp.where(is_fresh, values_img, key_block[1])
        image_next = combine(running_pair[0], block_stats(query_img, key_rows, values))
        text_next = combine(running_pair[1], block_stats(query_txt, key_block[0], key_block[1]))
        return ((image_next, text_next), None)

    result, _ = lax.scan(one_block, (image_init, text_init), (key_blocks, starts))
    image_total, text_total = result
    image_attn = finish(image_total)
    text_attn = finish(text_total)
    image_back, text_back = (
        lax.all_to_all(image_attn, "head", split_axis=0, concat_axis=1, tiled=True),
        lax.all_to_all(text_attn, "head", split_axis=0, concat_axis=1, tiled=True),
    )
    image_flat = image_back.reshape(img_rows, model_width)
    projected = jnp.dot(image_flat, proj_weight, preferred_element_type=jnp.float32)
    image_out = (residual.astype(jnp.float32) + gate_scale * projected).astype(jnp.bfloat16)
    return (image_out, text_back.reshape(text_back.shape[0], model_width))


def solution(mesh):
    return jax.shard_map(
        per_device,
        mesh=mesh,
        in_specs=(
            P(("patch", "head"), None),
            P("head", None),
            P(None, "patch", "head"),
            P(("patch", "head"), None),
            P(),
            P(),
        ),
        out_specs=(P(("patch", "head"), None), P("head", None)),
        check_vma=False,
    )
```

profile of v0, /device:TPU:96, one launch (start us, length us, event | category | flops | bytes accessed | tf_op | source)
XLA Modules:
  0.0 355.6 jit_solution(2656296785264345013)
XLA Ops:
  10.8 6.9 %all-to-all-start.1 = ((bf16[64,3,24,128]{3,0,1,2:T(8,128)(2,1)}), bf16[64,3,24,128]{3,0,1,2:T(8,128)(2,1)S(1)}, u32[]{:S(2)}, u32[]{:S(2)}) async-start(bf16[64,3,24,128]{3,0,1,2:T(8,128)(2,1)} %copy.82), calls=%async_computation.1 | async-start | bytes 2359296 | tf_op jit(solution)/shard_map/all_to_all | solution.py:46
  19.3 29.1 %all-to-all-done.1 = bf16[64,3,24,128]{3,0,1,2:T(8,128)(2,1)S(1)} async-done(((bf16[64,3,24,128]{3,0,1,2:T(8,128)(2,1)}), bf16[64,3,24,128]{3,0,1,2:T(8,128)(2,1)S(1)}, u32[]{:S(2)}, u32[]{:S(2)}) %all-to-all-start.1) | async-done | bytes 1179680 | tf_op jit(solution)/shard_map/all_to_all | solution.py:46
  48.3 4.3 %all-to-all-start = ((bf16[64,3,24,128]{3,0,1,2:T(8,128)(2,1)}), bf16[64,3,24,128]{3,0,1,2:T(8,128)(2,1)}, u32[]{:S(2)}, u32[]{:S(2)}) async-start(bf16[64,3,24,128]{3,0,1,2:T(8,128)(2,1)} %copy.79), calls=%async_computation | async-start | bytes 2359296 | tf_op jit(solution)/shard_map/all_to_all | solution.py:47
  52.7 30.9 %all-to-all-done = bf16[64,3,24,128]{3,0,1,2:T(8,128)(2,1)} async-done(((bf16[64,3,24,128]{3,0,1,2:T(8,128)(2,1)}), bf16[64,3,24,128]{3,0,1,2:T(8,128)(2,1)}, u32[]{:S(2)}, u32[]{:S(2)}) %all-to-all-start) | async-done | bytes 1179680 | tf_op jit(solution)/shard_map/all_to_all | solution.py:47
  94.2 2.9 fusion.49
  97.2 7.7 %all-gather.2.cloned.1.call-done = bf16[2,8192,384]{2,1,0:T(8,128)(2,1)} async-done(((bf16[2,512,384]{2,1,0:T(8,128)(2,1)}), bf16[2,8192,384]{2,1,0:T(8,128)(2,1)}) %all-gather.2.cloned.1.call-update) | async-done | bytes 12582928 | tf_op jit(solution)/shard_map/all_gather | solution.py:60
  104.9 16.7 %copy.87 = bf16[2,8192,384]{1,2,0:T(8,128)(2,1)} copy(bf16[2,8192,384]{2,1,0:T(8,128)(2,1)} %all-gather.2.cloned.1.call-done) | data formatting | bytes 25165824 | tf_op jit(solution)/shard_map/all_gather | solution.py:60
  121.6 12.8 %copy.109 = bf16[96,8,16,512]{3,2,1,0:T(8,128)(2,1)} copy(bf16[96,8,16,512]{3,1,2,0:T(8,128)(2,1)} %bitcast.177) | data formatting | bytes 25165824
  134.4 17.5 %copy.90 = bf16[16,2,512,3,128]{4,2,3,1,0:T(8,128)(2,1)} copy(bf16[16,2,512,3,128]{2,0,4,3,1:T(8,128)(2,1)} %bitcast.178) | data formatting | bytes 25165824 | tf_op jit(solution)/shard_map/while | solution.py:74
  152.0 149.5 %while.20 = (s32[]{:T(128)}, f32[512,3]{0,1:T(4,128)S(1)}, f32[512,3]{0,1:T(4,128)S(1)}, f32[512,3,128]{0,2,1:T(8,128)S(1)}, f32[512,3]{0,1:T(4,128)S(1)}, /*ind...) while((s32[]{:T(128)}, f32[512,3]{0,1:T(4,128)S(1)}, ...), condition=%wide.region_9.10_spmd, body=%wide.region_4.9_spmd.sunk | while | flops 819474432 | bytes 25338080 | solution.py:74
  159.4 1.9 fusion.90
  168.8 1.9 fusion.90
  178.1 1.9 fusion.90
  185.6 1.9 fusion.91
  187.4 1.9 fusion.90
  196.8 1.9 fusion.90
  206.1 1.9 fusion.90
  215.5 1.9 fusion.90
  224.8 1.9 fusion.90
  234.2 1.9 fusion.90
  243.5 1.9 fusion.90
  252.8 1.9 fusion.90
  262.2 1.9 fusion.90
  271.5 1.9 fusion.90
  280.9 1.9 fusion.90
  290.2 1.9 fusion.90
  299.6 1.9 fusion.90
  303.4 7.5 %all-to-all-start.3 = ((bf16[512,3,128]{2,1,0:T(4,128)(2,1)}), bf16[512,3,128]{2,1,0:T(4,128)(2,1)S(1)}, u32[]{:S(2)}, u32[]{:S(2)}) async-start(bf16[512,3,128]{2,1,0:T(4,128)(2,1)} %divide_convert_fusion), calls=%async_computation.3 | async-start | bytes 1048576 | tf_op jit(solution)/shard_map/all_to_all | solution.py:80
  312.9 10.0 %all-to-all-done.3 = bf16[512,3,128]{2,1,0:T(4,128)(2,1)S(1)} async-done(((bf16[512,3,128]{2,1,0:T(4,128)(2,1)}), bf16[512,3,128]{2,1,0:T(4,128)(2,1)S(1)}, u32[]{:S(2)}, u32[]{:S(2)}) %all-to-all-start.3) | async-done | bytes 393248 | tf_op jit(solution)/shard_map/all_to_all | solution.py:80
  323.0 3.7 %all-to-all-start.2 = ((bf16[512,3,128]{2,1,0:T(4,128)(2,1)}), bf16[512,3,128]{2,1,0:T(4,128)(2,1)S(1)}, u32[]{:S(2)}, u32[]{:S(2)}) async-start(bf16[512,3,128]{2,1,0:T(4,128)(2,1)} %divide_convert_fusion.1), calls=%async_computation.2 | async-start | bytes 1048576 | tf_op jit(solution)/shard_map/all_to_all | solution.py:79
  328.1 9.3 %all-to-all-done.2 = bf16[512,3,128]{2,1,0:T(4,128)(2,1)S(1)} async-done(((bf16[512,3,128]{2,1,0:T(4,128)(2,1)}), bf16[512,3,128]{2,1,0:T(4,128)(2,1)S(1)}, u32[]{:S(2)}, u32[]{:S(2)}) %all-to-all-start.2) | async-done | bytes 393248 | tf_op jit(solution)/shard_map/all_to_all | solution.py:79
  338.2 10.5 %fusion.45 = bf16[64,3072]{1,0:T(8,128)(2,1)} fusion(bf16[64,3072]{1,0:T(8,128)(2,1)S(1)} %reshape.39, bf16[3072,3072]{1,0:T(8,128)(2,1)} %param.13, bf16[64,3072]{1,0:T(8,128)(2,1)S(1)} %copy-done.6, f32[3072]{0:T(1024)S(1)} %copy-done.7), kind=kOutput, calls=%fused_computation.44 | convolution fusion | flops 1208745984 | bytes 20066304 | tf_op jit(solution)/shard_map/dot_general | solution.py:83
  (155 shorter events, 128.4 us)
Async XLA Ops:
  7.2 97.8 %all-gather.2.cloned.1.call-start = ((), (), s32[]{:S(2)}) async-start(), calls=%async_computation.4 | async-start | bytes 13369344 | tf_op jit(solution)/shard_map/all_gather | solution.py:60
  7.9 9.8 %copy-start.5 = (bf16[64,9216]{1,0:T(8,128)(2,1)S(1)}, bf16[64,9216]{1,0:T(8,128)(2,1)}, u32[]{:S(2)}) copy-start(bf16[64,9216]{1,0:T(8,128)(2,1)} %param.9) | copy-start | bytes 3538948
  10.8 37.5 %all-to-all-start.1 = ((bf16[64,3,24,128]{3,0,1,2:T(8,128)(2,1)}), bf16[64,3,24,128]{3,0,1,2:T(8,128)(2,1)S(1)}, u32[]{:S(2)}, u32[]{:S(2)}) async-start(bf16[64,3,24,128]{3,0,1,2:T(8,128)(2,1)} %copy.82), calls=%async_computation.1 | async-start | bytes 2359296 | tf_op jit(solution)/shard_map/all_to_all | solution.py:46
  48.3 35.3 %all-to-all-start = ((bf16[64,3,24,128]{3,0,1,2:T(8,128)(2,1)}), bf16[64,3,24,128]{3,0,1,2:T(8,128)(2,1)}, u32[]{:S(2)}, u32[]{:S(2)}) async-start(bf16[64,3,24,128]{3,0,1,2:T(8,128)(2,1)} %copy.79), calls=%async_computation | async-start | bytes 2359296 | tf_op jit(solution)/shard_map/all_to_all | solution.py:47
  52.7 32.9 %copy-start.4 = (bf16[8,64,3,3,128]{4,1,0,3,2:T(8,128)(2,1)}, bf16[8,64,3,3,128]{4,1,0,3,2:T(8,128)(2,1)S(1)}, u32[]{:S(2)}) copy-start(bf16[8,64,3,3,128]{4,1,0,3,2:T(8,128)(2,1)S(1)} %copy.84) | copy-start | bytes 3538948
  85.0 4.0 %copy-start.3 = (bf16[8,64,3,3,128]{4,1,0,3,2:T(8,128)(2,1)}, bf16[8,64,3,3,128]{4,1,0,3,2:T(8,128)(2,1)S(1)}, u32[]{:S(2)}) copy-start(bf16[8,64,3,3,128]{4,1,0,3,2:T(8,128)(2,1)S(1)} %copy.81) | copy-start | bytes 3538948
  85.6 1.6 copy-start
  89.0 1.6 copy-start.2
  91.8 2.5 copy-start.1
  303.4 19.5 %all-to-all-start.3 = ((bf16[512,3,128]{2,1,0:T(4,128)(2,1)}), bf16[512,3,128]{2,1,0:T(4,128)(2,1)S(1)}, u32[]{:S(2)}, u32[]{:S(2)}) async-start(bf16[512,3,128]{2,1,0:T(4,128)(2,1)} %divide_convert_fusion), calls=%async_computation.3 | async-start | bytes 1048576 | tf_op jit(solution)/shard_map/all_to_all | solution.py:80
  312.9 25.3 %copy-start.6 = (bf16[64,3072]{1,0:T(8,128)(2,1)S(1)}, bf16[64,3072]{1,0:T(8,128)(2,1)}, u32[]{:S(2)}) copy-start(bf16[64,3072]{1,0:T(8,128)(2,1)} %param.11) | copy-start | bytes 1179652
  312.9 25.3 %copy-start.7 = (f32[3072]{0:T(1024)S(1)}, f32[3072]{0:T(1024)}, u32[]{:S(2)}) copy-start(f32[3072]{0:T(1024)} %param.12) | copy-start | bytes 36868
  323.0 14.5 %all-to-all-start.2 = ((bf16[512,3,128]{2,1,0:T(4,128)(2,1)}), bf16[512,3,128]{2,1,0:T(4,128)(2,1)S(1)}, u32[]{:S(2)}, u32[]{:S(2)}) async-start(bf16[512,3,128]{2,1,0:T(4,128)(2,1)} %divide_convert_fusion.1), calls=%async_computation.2 | async-start | bytes 1048576 | tf_op jit(solution)/shard_map/all_to_all | solution.py:79
Sparse Core Ops, SparseCore 0:
  9.6 95.2 all-gather.1
where the time goes:
time: 360 us; the launch traced here: 356 us
  matrix products  125 us (35%)
  waiting for transfers between devices  87.7 us (24%)
  local copies, waits for them, and re-layouts  72.4 us (20%)
  other arithmetic  23.4 us (6%)
  starting transfers between devices  22.4 us (6%)
  between operations  14.3 us (4%)
  loops' own time  10.8 us (3%)
    dot_general x34, matrix products, block_stats(): jnp.einsum('rhk,khd->rhd', shifted.astype(jnp.bfloat16), values, preferre...  62.2 us
    dot_general x34, matrix products, block_stats(): jnp.einsum('rhd,khd->rhk', queries, key_rows, preferred_element_type=jnp....  51.9 us
    all_to_all x1, waiting for transfers between devices, per_device(): lax.all_to_all(txt_split, 'head', split_axis=2, concat_axis=0, tiled=True)  30.9 us
    all_to_all x1, waiting for transfers between devices, per_device(): lax.all_to_all(img_split, 'head', split_axis=2, concat_axis=0, tiled=True)  29.1 us
    reduce_sum x33, other arithmetic, block_stats(): row_sum = jnp.sum(shifted, axis=2)  20 us
    while x7, local copies, waits for them, and re-layouts, per_device(): lax.scan(one_block, (image_init, text_init), (key_blocks, starts))  19.1 us
    unnamed x19, local copies, waits for them, and re-layouts  18.7 us
    all_gather x1, local copies, waits for them, and re-layouts, per_device(): shard_rows = lax.all_gather(stale_kv, 'patch', axis=1, tiled=True)  16.7 us
  transfers between devices with their start and end apart: 5, of which 5 were waited for; matrix products, arithmetic and copies ran while one was open for 5% of the time, Pallas kernels for 0%

commit v1 on v0

--- a/solution.py
+++ b/solution.py
@@ -57,7 +57,10 @@
     image_init = block_stats(query_img, keys_txt, values_txt)
     text_init = block_stats(query_txt, keys_txt, values_txt)
     own_first = my_group * group_rows
-    shard_rows = lax.all_gather(stale_kv, "patch", axis=1, tiled=True)
+    known = jax.lax.axis_size("patch")
+    all_rows = jnp.stack([stale_kv] * known)
+    new = jax.lax.all_to_all(all_rows, split_axis=0, concat_axis=0, axis_name="patch")
+    shard_rows = jnp.concatenate(new, axis=1)
     shard_count = shard_rows.shape[1] // group_rows
     key_blocks = jnp.moveaxis(shard_rows.reshape(2, shard_count, group_rows, local_heads, HD), 1, 0)
     starts = group_rows * jnp.arange(shard_count, dtype=jnp.int32)

time: 360 us -> 481 us (1.34)
  waiting for transfers between devices: 87.7 us -> 168 us
  local copies, waits for them, and re-layouts: 72.4 us -> 110 us
  other arithmetic: 23.4 us -> 44 us
  between operations: 14.3 us -> 0.84 us
  matrix products: 125 us -> 118 us
    all_to_all x0 -> x1, waiting for transfers between devices: none -> 116 us  [per_device(): jax.lax.all_to_all(all_rows, split_axis=0, concat_axis=0, axis_name='patch')]
    while x0 -> x320, local copies, waits for them, and re-layouts: none -> 45.1 us
    add x16, other arithmetic: 0.58 us -> 21.2 us  [combine(): first[1] * first_scale + second[1] * second_scale]
    slice x0 -> x16, local copies, waits for them, and re-layouts: none -> 18.6 us  [one_block(): values = jnp.where(is_fresh, values_img, key_block[1])]
    all_gather x1 -> x0, local copies, waits for them, and re-layouts: 16.7 us -> none  [per_device(): shard_rows = lax.all_gather(stale_kv, 'patch', axis=1, tiled=True)]
    all_to_all x1, waiting for transfers between devices: 30.9 us -> 17.1 us  [per_device(): lax.all_to_all(txt_split, 'head', split_axis=2, concat_axis=0, tiled=True)]
    unnamed x19 -> x21, local copies, waits for them, and re-layouts: 18.7 us -> 6.03 us
    all_to_all x1, waiting for transfers between devices: 29.1 us -> 16.5 us  [per_device(): lax.all_to_all(img_split, 'head', split_axis=2, concat_axis=0, tiled=True)]
where the time goes in v1:
time: 481 us; the launch traced here: 475 us
  waiting for transfers between devices  168 us (35%)
  matrix products  118 us (25%)
  local copies, waits for them, and re-layouts  110 us (23%)
  other arithmetic  44 us (9%)
  starting transfers between devices  22.7 us (5%)
  loops' own time  11.1 us (2%)
    all_to_all x1, waiting for transfers between devices, per_device(): jax.lax.all_to_all(all_rows, split_axis=0, concat_axis=0, axis_name='patch')  116 us
    dot_general x34, matrix products, block_stats(): jnp.einsum('rhk,khd->rhd', shifted.astype(jnp.bfloat16), values, preferre...  65.7 us
    while x320, local copies, waits for them, and re-layouts  45.1 us
    dot_general x34, matrix products, block_stats(): jnp.einsum('rhd,khd->rhk', queries, key_rows, preferred_element_type=jnp....  42.2 us
    add x16, other arithmetic, combine(): first[1] * first_scale + second[1] * second_scale  21.2 us
    reduce_sum x33, other arithmetic, block_stats(): row_sum = jnp.sum(shifted, axis=2)  19.4 us
    dynamic_slice x16, local copies, waits for them, and re-layouts, per_device(): lax.scan(one_block, (image_init, text_init), (key_blocks, starts))  18.9 us
    slice x16, local copies, waits for them, and re-layouts, one_block(): values = jnp.where(is_fresh, values_img, key_block[1])  18.6 us
  transfers between devices with their start and end apart: 5, of which 5 were waited for; matrix products, arithmetic and copies ran while one was open for 5% of the time, Pallas kernels for 0%

profile of v1, /device:TPU:96, one launch (start us, length us, event | category | flops | bytes accessed | tf_op | source)
XLA Modules:
  0.0 475.0 jit_solution(3436450128798746405)
XLA Ops:
  3.5 6.9 %all-to-all-start = ((bf16[64,3,24,128]{3,0,1,2:T(8,128)(2,1)}), bf16[64,3,24,128]{3,0,1,2:T(8,128)(2,1)S(1)}, u32[]{:S(2)}, u32[]{:S(2)}) async-start(bf16[64,3,24,128]{3,0,1,2:T(8,128)(2,1)} %copy.80), calls=%async_computation | async-start | bytes 2359296 | tf_op jit(solution)/shard_map/all_to_all | solution.py:47
  12.0 17.1 %all-to-all-done = bf16[64,3,24,128]{3,0,1,2:T(8,128)(2,1)S(1)} async-done(((bf16[64,3,24,128]{3,0,1,2:T(8,128)(2,1)}), bf16[64,3,24,128]{3,0,1,2:T(8,128)(2,1)S(1)}, u32[]{:S(2)}, u32[]{:S(2)}) %all-to-all-start) | async-done | bytes 1179680 | tf_op jit(solution)/shard_map/all_to_all | solution.py:47
  29.1 3.6 all-to-all-start.1
  34.1 16.5 %all-to-all-done.1 = bf16[64,3,24,128]{3,0,1,2:T(8,128)(2,1)S(1)} async-done(((bf16[64,3,24,128]{3,0,1,2:T(8,128)(2,1)}), bf16[64,3,24,128]{3,0,1,2:T(8,128)(2,1)S(1)}, u32[]{:S(2)}, u32[]{:S(2)}) %all-to-all-start.1) | async-done | bytes 1179680 | tf_op jit(solution)/shard_map/all_to_all | solution.py:46
  50.6 5.9 %stack.2 = bf16[16,2,512,384]{2,3,1,0:T(8,128)(2,1)} broadcast(bf16[2,512,384]{1,2,0:T(8,128)(2,1)S(1)} %copy.88), dimensions={1,2,3} | broadcast | bytes 13369344 | tf_op jit(solution)/shard_map/stack | solution.py:61
  56.5 5.0 %all-to-all-start.2 = ((bf16[16,2,512,384]{2,3,1,0:T(8,128)(2,1)}), bf16[16,2,512,384]{2,3,1,0:T(8,128)(2,1)}, u32[]{:S(2)}, u32[]{:S(2)}) async-start(bf16[16,2,512,384]{2,3,1,0:T(8,128)(2,1)} %stack.2), calls=%async_computation.2 | async-start | bytes 25165824 | tf_op jit(solution)/shard_map/all_to_all | solution.py:62
  64.6 2.5 fusion.56
  73.4 2.8 fusion.59
  78.5 2.7 slice_bitcast_fusion
  83.6 116.1 %all-to-all-done.2 = bf16[16,2,512,384]{2,3,1,0:T(8,128)(2,1)} async-done(((bf16[16,2,512,384]{2,3,1,0:T(8,128)(2,1)}), bf16[16,2,512,384]{2,3,1,0:T(8,128)(2,1)}, u32[]{:S(2)}, u32[]{:S(2)}) %all-to-all-start.2) | async-done | bytes 12582944 | tf_op jit(solution)/shard_map/all_to_all | solution.py:62
  199.7 231.0 %while.20 = (s32[]{:T(128)}, f32[512,3]{0,1:T(4,128)}, f32[512,3]{0,1:T(4,128)}, f32[512,3,128]{0,2,1:T(8,128)}, f32[512,3]{0,1:T(4,128)}, /*index=5*/f32[512,3]...) while((s32[]{:T(128)}, f32[512,3]{0,1:T(4,128)}, ...), condition=%wide.region_9.10_spmd, body=%wide.region_4.9_spmd.sunk | while | flops 819474432 | bytes 39592388 | solution.py:77
  211.3 2.9 fusion.86
  225.7 2.9 fusion.86
  240.1 2.9 fusion.86
  254.5 2.9 fusion.86
  269.0 2.9 fusion.86
  283.4 2.9 fusion.86
  297.8 2.9 fusion.86
  312.2 2.9 fusion.86
  326.7 2.9 fusion.86
  341.1 2.9 fusion.86
  355.5 2.9 fusion.86
  369.9 2.9 fusion.86
  384.5 3.0 fusion.86
  399.0 2.9 fusion.86
  413.4 2.9 fusion.86
  427.9 2.9 fusion.86
  434.6 3.5 all-to-all-start.4
  440.1 9.5 %all-to-all-done.4 = bf16[512,3,128]{2,1,0:T(4,128)(2,1)S(1)} async-done(((bf16[512,3,128]{2,1,0:T(4,128)(2,1)}), bf16[512,3,128]{2,1,0:T(4,128)(2,1)S(1)}, u32[]{:S(2)}, u32[]{:S(2)}) %all-to-all-start.4) | async-done | bytes 393248 | tf_op jit(solution)/shard_map/all_to_all | solution.py:83
  449.6 3.7 all-to-all-start.3
  454.8 8.9 %all-to-all-done.3 = bf16[512,3,128]{2,1,0:T(4,128)(2,1)S(1)} async-done(((bf16[512,3,128]{2,1,0:T(4,128)(2,1)}), bf16[512,3,128]{2,1,0:T(4,128)(2,1)S(1)}, u32[]{:S(2)}, u32[]{:S(2)}) %all-to-all-start.3) | async-done | bytes 393248 | tf_op jit(solution)/shard_map/all_to_all | solution.py:82
  464.5 10.5 %fusion.41 = bf16[64,3072]{1,0:T(8,128)(2,1)} fusion(bf16[64,3072]{1,0:T(8,128)(2,1)S(1)} %reshape.41, bf16[3072,3072]{1,0:T(8,128)(2,1)} %param.13, bf16[64,3072]{1,0:T(8,128)(2,1)S(1)} %copy-done.16, f32[3072]{0:T(1024)S(1)} %copy-done.17), kind=kOutput, calls=%fused_computation.42 | convolution fusion | flops 1208745984 | bytes 20066304 | tf_op jit(solution)/shard_map/dot_general | solution.py:86
  (491 shorter events, 201.8 us)
Async XLA Ops:
  0.6 9.8 %copy-start.10 = (bf16[64,9216]{1,0:T(8,128)(2,1)S(1)}, bf16[64,9216]{1,0:T(8,128)(2,1)}, u32[]{:S(2)}) copy-start(bf16[64,9216]{1,0:T(8,128)(2,1)} %param.8) | copy-start | bytes 3538948
  3.5 25.6 %all-to-all-start = ((bf16[64,3,24,128]{3,0,1,2:T(8,128)(2,1)}), bf16[64,3,24,128]{3,0,1,2:T(8,128)(2,1)S(1)}, u32[]{:S(2)}, u32[]{:S(2)}) async-start(bf16[64,3,24,128]{3,0,1,2:T(8,128)(2,1)} %copy.80), calls=%async_computation | async-start | bytes 2359296 | tf_op jit(solution)/shard_map/all_to_all | solution.py:47
  29.1 21.5 %all-to-all-start.1 = ((bf16[64,3,24,128]{3,0,1,2:T(8,128)(2,1)}), bf16[64,3,24,128]{3,0,1,2:T(8,128)(2,1)S(1)}, u32[]{:S(2)}, u32[]{:S(2)}) async-start(bf16[64,3,24,128]{3,0,1,2:T(8,128)(2,1)} %copy.83), calls=%async_computation.1 | async-start | bytes 2359296 | tf_op jit(solution)/shard_map/all_to_all | solution.py:46
  56.5 143.2 %all-to-all-start.2 = ((bf16[16,2,512,384]{2,3,1,0:T(8,128)(2,1)}), bf16[16,2,512,384]{2,3,1,0:T(8,128)(2,1)}, u32[]{:S(2)}, u32[]{:S(2)}) async-start(bf16[16,2,512,384]{2,3,1,0:T(8,128)(2,1)} %stack.2), calls=%async_computation.2 | async-start | bytes 25165824 | tf_op jit(solution)/shard_map/all_to_all | solution.py:62
  78.5 2.7 copy-start.6
  200.9 2.7 copy-start
  215.3 2.7 copy-start
  220.4 2.5 copy-start.2
  229.7 2.7 copy-start
  234.8 2.5 copy-start.2
  244.1 2.7 copy-start
  249.2 2.5 copy-start.2
  258.6 2.7 copy-start
  273.0 2.7 copy-start
  278.1 2.5 copy-start.2
  287.4 2.7 copy-start
  292.5 2.5 copy-start.2
  301.8 2.7 copy-start
  316.3 2.7 copy-start
  330.7 2.7 copy-start
  345.1 2.7 copy-start
  359.5 2.7 copy-start
  374.0 2.7 copy-start
  388.6 2.7 copy-start
  403.0 2.7 copy-start
  417.5 2.7 copy-start
  430.7 7.4 %copy-start.4 = (f32[512,3,128]{0,2,1:T(8,128)S(1)}, f32[512,3,128]{0,2,1:T(8,128)}, u32[]{:S(2)}) copy-start(f32[512,3,128]{0,2,1:T(8,128)} %get-tuple-element.77) | copy-start | bytes 2359300
  430.7 7.8 %copy-start.13 = (f32[512,3]{0,1:T(4,128)S(1)}, f32[512,3]{0,1:T(4,128)}, u32[]{:S(2)}) copy-start(f32[512,3]{0,1:T(4,128)} %get-tuple-element.78) | copy-start | bytes 18436
  434.6 15.0 %all-to-all-start.4 = ((bf16[512,3,128]{2,1,0:T(4,128)(2,1)}), bf16[512,3,128]{2,1,0:T(4,128)(2,1)S(1)}, u32[]{:S(2)}, u32[]{:S(2)}) async-start(bf16[512,3,128]{2,1,0:T(4,128)(2,1)} %divide_convert_fusion), calls=%async_computation.4 | async-start | bytes 1048576 | tf_op jit(solution)/shard_map/all_to_all | solution.py:83
  440.1 24.4 %copy-start.16 = (bf16[64,3072]{1,0:T(8,128)(2,1)S(1)}, bf16[64,3072]{1,0:T(8,128)(2,1)}, u32[]{:S(2)}) copy-start(bf16[64,3072]{1,0:T(8,128)(2,1)} %param.11) | copy-start | bytes 1179652
  440.1 24.4 %copy-start.17 = (f32[3072]{0:T(1024)S(1)}, f32[3072]{0:T(1024)}, u32[]{:S(2)}) copy-start(f32[3072]{0:T(1024)} %param.12) | copy-start | bytes 36868
  449.6 14.2 %all-to-all-start.3 = ((bf16[512,3,128]{2,1,0:T(4,128)(2,1)}), bf16[512,3,128]{2,1,0:T(4,128)(2,1)S(1)}, u32[]{:S(2)}, u32[]{:S(2)}) async-start(bf16[512,3,128]{2,1,0:T(4,128)(2,1)} %divide_convert_fusion.1), calls=%async_computation.3 | async-start | bytes 1048576 | tf_op jit(solution)/shard_map/all_to_all | solution.py:82
  (126 other events, 218.9 us)
